TPU v7x, 32 devices: a whole 2x2x4 slice. The times are simulated.
32 devices in a mesh: seq: 8 (over y, x, core), batch: 4 (over z).
Axes of the slice: x: 2, y: 2, z: 4, core: 2. Of those that a mesh axis runs over, the one named last changes fastest.
Arguments:
- tokens: bfloat16 [4, 4096, 2048], P('batch', 'seq'), may hold values from -6 to 6
- w_qkv: bfloat16 [2048, 3072], replicated, may hold values from -0.125 to 0.125
- cotangent: bfloat16 [4, 4096, 1024], P('batch', 'seq'), may hold values from -6 to 6
Outputs:
- attended: bfloat16 [4, 4096, 1024], P('batch', 'seq')
- token_grad: bfloat16 [4, 4096, 2048], P('batch', 'seq')
- weight_grad: float32 [2048, 3072], P('seq')
All inputs are finite; a program needn't handle non-finite values.
Results may differ from a plain program's by a relative error of at most 0.0064.
Values sent between devices are 32-bit elements; how exact they have to be, the bound alone decides.
A program may use at most 192 MiB of HBM per device.

v0:
```python
import jax
import jax.numpy as jnp
from jax import lax
from jax.sharding import PartitionSpec as P

HEADS = 8
DH = 128
BLK = 512


PRECISE = lax.Precision.HIGHEST


def running_states(block_states, incoming, reverse):
    zero_block = jnp.zeros_like(block_states)
    if reverse:
        totals = jnp.cumsum(block_states[::-1], axis=0)[::-1]
        return incoming[None] + jnp.concatenate([totals[1:], zero_block], 0)
    totals = jnp.cumsum(block_states, axis=0)
    return incoming[None] + jnp.concatenate([zero_block, totals[:-1]], 0)


def body(tokens, w_qkv, cotangent):
    row_count = tokens.shape[1]
    width = w_qkv.shape[1] // 3
    block_count = row_count // BLK
    seq_count = lax.axis_size("seq")
    batch_count = lax.axis_size("batch")
    local_x = tokens[0]
    projected = jnp.dot(local_x, w_qkv, preferred_element_type=jnp.float32).astype(jnp.bfloat16)
    queries = projected[:, :width].reshape(block_count, BLK, HEADS, DH)
    key_heads = projected[:, width : 2 * width].reshape(block_count, BLK, HEADS, DH)
    value_heads = projected[:, 2 * width :].reshape(block_count, BLK, HEADS, DH)
    position = lax.axis_index("seq") * row_count + jnp.arange(row_count, dtype=jnp.int32)
    pos_scale = DH ** (-0.5) / jnp.sqrt(position.astype(jnp.float32) + 1.0)
    scaled_grad = (cotangent[0].astype(jnp.float32) * pos_scale[:, None]).astype(jnp.bfloat16)
    grad_heads = scaled_grad.reshape(block_count, BLK, HEADS, DH)
    kv_blocks = jnp.einsum(
        "nrha,nrhb->nhab", key_heads, value_heads, preferred_element_type=jnp.float32
    )
    grad_blocks = jnp.einsum(
        "nrha,nrhb->nhab", queries, grad_heads, preferred_element_type=jnp.float32
    )
    kv_local = jnp.sum(kv_blocks, 0)
    grad_local = jnp.sum(grad_blocks, 0)
    kv_all, grad_all = (
        lax.all_gather(kv_local[None], "seq", axis=0, tiled=True),
        lax.all_gather(grad_local[None], "seq", axis=0, tiled=True),
    )
    rank_list = jnp.arange(seq_count, dtype=jnp.int32)
    my_rank = lax.axis_index("seq")
    kv_in = jnp.sum(jnp.where((rank_list < my_rank)[:, None, None, None], kv_all, 0.0), 0)
    grad_in = jnp.sum(jnp.where((rank_list > my_rank)[:, None, None, None], grad_all, 0.0), 0)
    kv_before = running_states(kv_blocks, kv_in, False)
    grad_after = running_states(grad_blocks, grad_in, True)
    causal = jnp.arange(BLK)[:, None] >= jnp.arange(BLK)[None, :]
    scores = jnp.where(
        causal,
        jnp.einsum("nihd,njhd->nhij", queries, key_heads, preferred_element_type=jnp.float32),
        0.0,
    ).astype(jnp.bfloat16)
    grad_scores = jnp.where(
        causal,
        jnp.einsum("nihd,njhd->nhij", grad_heads, value_heads, preferred_element_type=jnp.float32),
        0.0,
    ).astype(jnp.bfloat16)
    query_wide = queries.astype(jnp.float32)
    key_wide = key_heads.astype(jnp.float32)
    value_wide = value_heads.astype(jnp.float32)
    grad_wide = grad_heads.astype(jnp.float32)
    attended = jnp.einsum(
        "nhij,njhd->nihd", scores, value_heads, preferred_element_type=jnp.float32
    )
    attended = attended + jnp.einsum("nihd,nhde->nihe", query_wide, kv_before, precision=PRECISE)
    attended = attended * pos_scale.reshape(block_count, BLK, 1, 1)
    query_grad = jnp.einsum(
        "nhij,njhd->nihd", grad_scores, key_heads, preferred_element_type=jnp.float32
    )
    query_grad = query_grad + jnp.einsum("nihe,nhde->nihd", grad_wide, kv_before, precision=PRECISE)
    key_grad = jnp.einsum(
        "nhij,nihd->njhd", grad_scores, queries, preferred_element_type=jnp.float32
    )
    key_grad = key_grad + jnp.einsum("njhe,nhde->njhd", value_wide, grad_after, precision=PRECISE)
    value_grad = jnp.einsum(
        "nhij,nihe->njhe", scores, grad_heads, preferred_element_type=jnp.float32
    )
    value_grad = value_grad + jnp.einsum("njhd,nhde->njhe", key_wide, grad_after, precision=PRECISE)
    qkv_grad = jnp.concatenate(
        [
            query_grad.reshape(row_count, width),
            key_grad.reshape(row_count, width),
            value_grad.reshape(row_count, width),
        ],
        1,
    ).astype(jnp.bfloat16)
    token_grad = lax.dot_general(
        qkv_grad, w_qkv, (((1,), (1,)), ((), ())), preferred_element_type=jnp.float32
    )
    token_grad = token_grad.astype(jnp.bfloat16)[None]
    partial_rows = lax.psum_scatter(
        lax.dot_general(
            local_x, qkv_grad, (((0,), (0,)), ((), ())), preferred_element_type=jnp.float32
        ),
        "seq",
        scatter_dimension=0,
        tiled=True,
    )
    summed = lax.psum(partial_rows, "batch")
    grad_scale = 1.0 / jnp.sqrt(jnp.float32(batch_count * seq_count * row_count))
    weight_grad = summed * grad_scale
    return (attended.reshape(row_count, width).astype(jnp.bfloat16)[None], token_grad, weight_grad)


def solution(mesh):
    return jax.shard_map(
        body,
        mesh=mesh,
        in_specs=(P("batch", "seq", None), P(), P("batch", "seq", None)),
        out_specs=(P("batch", "seq", None), P("batch", "seq", None), P("seq", None)),
        check_vma=False,
    )
```

profile of v0, /device:TPU:0, one launch (start us, length us, event | category | flops | bytes accessed | tf_op | source)
XLA Modules:
  0.0 420.3 jit_solution(13077857208843234971)
XLA Ops:
  7.2 0.0 copy-start
  7.2 0.0 all-gather.7.cloned.1.call-start
  7.2 2.7 copy.51
  10.0 0.0 copy-done
  10.0 9.6 %convolution_convert_fusion = bf16[512,3072]{1,0:T(8,128)(2,1)S(1)} fusion(bf16[2048,3072]{1,0:T(8,128)(2,1)} %param.4, bf16[1,512,2048]{2,1,0:T(8,128)(2,1)S(1)} %copy-done), kind=kOutput, calls=%fused_computation.3 | convolution fusion | flops 6444023808 | bytes 17825792 | tf_op jit(solution)/shard_map/dot_general | solution.py:30
  19.6 2.2 slice_bitcast_fusion.2
  21.8 2.3 copy.52
  24.1 2.0 multiply_convert_fusion
  26.0 0.0 copy-start.6
  26.0 1.0 copy-done.6
  27.1 0.0 copy-done.3
  27.1 1.2 fusion.22
  28.3 0.0 all-gather.7.cloned.1.call-update
  28.3 0.0 all-gather.5.cloned.1.call-start
  28.4 2.5 copy.55
  30.9 2.4 copy.29
  33.3 2.5 fusion.10
  35.7 0.0 all-gather.5.cloned.1.call-update
  35.8 0.2 reduce-scatter.2.cloned.1.call-start
  36.0 0.1 iota_compare_fusion
  36.1 0.0 copy-start.4
  36.1 0.0 copy-start.15
  36.1 2.8 select_convert_fusion
  38.9 0.0 copy-done.4
  38.9 0.0 copy-done.15
  38.9 1.5 select_convert_fusion.1
  40.4 0.0 copy-start.2
  40.4 0.0 copy-start.9
  40.4 2.0 fusion.21
  42.5 0.0 copy-done.9
  42.5 2.9 fusion.20
  45.4 0.0 copy-done.2
  45.4 0.0 copy-done.7
  45.4 2.0 fusion.23
  47.4 20.4 %all-gather.7.cloned.1.call-done = f32[64,128,128]{2,1,0:T(8,128)} async-done(((f32[8,128,128]{2,1,0:T(8,128)}), f32[64,128,128]{2,1,0:T(8,128)}) %all-gather.7.cloned.1.call-update) | async-done | bytes 4194320 | tf_op jit(solution)/shard_map/all_gather | solution.py:48
  67.8 2.9 select_reduce_fusion
  70.7 0.0 copy-done.12
  70.7 0.2 copy-done.16
  70.9 2.2 add_convert_fusion
  73.1 0.0 copy-done.11
  73.1 2.1 add_convert_fusion.1
  75.2 31.1 %all-gather.5.cloned.1.call-done = f32[64,128,128]{2,1,0:T(8,128)} async-done(((f32[8,128,128]{2,1,0:T(8,128)}), f32[64,128,128]{2,1,0:T(8,128)}) %all-gather.5.cloned.1.call-update) | async-done | bytes 4194320 | tf_op jit(solution)/shard_map/all_gather | solution.py:47
  106.3 2.9 select_reduce_fusion.1
  109.2 0.0 copy-done.8
  109.2 0.3 copy-done.10
  109.5 1.1 add_convert_fusion.2
  110.6 0.0 copy-done.13
  110.7 1.0 copy-done.19
  111.6 15.2 %convolution_bitcast_fusion = f32[2048,3072]{0,1:T(8,128)} fusion(bf16[1,512,2048]{2,1,0:T(8,128)(2,1)S(1)} %copy-done, bf16[512,1024]{0,1:T(8,128)(2,1)S(1)} %bitcast.86, bf16[512,1024]{0,1:T(8,128)(2,1)S(1)} %bitcast.88, bf16[512,1024]{0,1:T(8,128)(2,1)S(1)} %bitcast.89), kind=kOutput, calls=%fused_computation | convolution fusion | flops 6451888128 | bytes 30408704 | tf_op jit(solution)/shard_map/dot_general | solution.py:101
  126.8 0.0 reduce-scatter.2.cloned.1.call-update
  126.8 0.0 all-reduce.2.cloned.1.call-start
  126.9 156.1 %reduce-scatter.2.cloned.1.call-done = f32[256,3072]{0,1:T(8,128)} async-done(((f32[2048,3072]{0,1:T(8,128)}), f32[256,3072]{0,1:T(8,128)}) %reduce-scatter.2.cloned.1.call-update) | async-done | bytes 3145744 | tf_op jit(solution)/shard_map/reduce_scatter | solution.py:100
  283.0 0.0 all-reduce.2.cloned.1.call-update
  283.0 0.0 copy-start.14
  283.0 3.8 fusion.6
  286.8 0.0 copy-done.5
  286.9 0.0 copy-done.14
  286.9 1.1 fusion.1
  288.0 1.3 copy.44
  289.3 13.6 %fusion = bf16[1,512,2048]{2,1,0:T(8,128)(2,1)} fusion(bf16[2048,3072]{1,0:T(8,128)(2,1)} %param.4, bf16[512,1024]{0,1:T(8,128)(2,1)} %bitcast.85, bf16[512,1024]{0,1:T(8,128)(2,1)} %bitcast.87, bf16[512,1024]{0,1:T(8,128)(2,1)} %bitcast.90), kind=kOutput, calls=%fused_computation.8 | convolution fusion | flops 6452936704 | bytes 17825792 | tf_op jit(solution)/shard_map/dot_general | solution.py:96
  302.9 103.4 %all-reduce.2.cloned.1.call-done = f32[256,3072]{0,1:T(8,128)} async-done(((f32[256,3072]{0,1:T(8,128)}), f32[256,3072]{0,1:T(8,128)}) %all-reduce.2.cloned.1.call-update) | async-done | bytes 3145744 | tf_op jit(solution)/shard_map/psum | solution.py:108
  406.3 3.9 broadcast_multiply_fusion
  410.2 3.5 copy.45
  413.7 0.0 copy-done.1
  (18 shorter events, 0.0 us)
Async XLA Ops:
  7.2 2.8 copy-start
  7.2 60.6 %all-gather.7.cloned.1.call-start = ((), (), s32[]{:S(2)}) async-start(), calls=%async_computation.4 | async-start | bytes 4718592 | tf_op jit(solution)/shard_map/all_gather | solution.py:48
  24.1 3.0 copy-start.3
  26.0 1.0 copy-start.6
  28.3 78.0 %all-gather.5.cloned.1.call-start = ((), (), s32[]{:S(2)}) async-start(), calls=%async_computation.3 | async-start | bytes 4718592 | tf_op jit(solution)/shard_map/all_gather | solution.py:47
  35.8 247.2 %reduce-scatter.2.cloned.1.call-start = ((), (), s32[]{:S(2)}) async-start(), calls=%async_computation.1 | async-start | bytes 28311552 | tf_op jit(solution)/shard_map/reduce_scatter | solution.py:100
  36.1 2.8 copy-start.4
  36.1 2.8 copy-start.15
  40.4 4.9 %copy-start.2 = (bf16[8,512,512]{2,1,0:T(8,128)(2,1)}, bf16[8,512,512]{2,1,0:T(8,128)(2,1)S(1)}, u32[]{:S(2)}) copy-start(bf16[8,512,512]{2,1,0:T(8,128)(2,1)S(1)} %select_convert_fusion.1) | copy-start | bytes 12582916
  40.4 2.0 copy-start.9
  42.5 2.9 copy-start.7
  67.8 2.9 copy-start.12
  67.8 3.1 copy-start.16
  70.9 2.2 copy-start.11
  106.3 2.9 copy-start.8
  106.3 3.2 copy-start.10
  109.5 1.2 copy-start.13
  109.5 2.1 copy-start.17
  109.5 2.1 copy-start.18
  110.7 1.0 copy-start.19
  126.8 279.5 %all-reduce.2.cloned.1.call-start = ((), (), s32[]{:S(2)}) async-start(), calls=%async_computation.2 | async-start | bytes 6291456 | tf_op jit(solution)/shard_map/psum | solution.py:108
  283.0 3.8 copy-start.5
  283.0 3.8 copy-start.14
  406.3 7.5 %copy-start.1 = (bf16[1,512,2048]{2,1,0:T(8,128)(2,1)S(1)}, bf16[1,512,2048]{2,1,0:T(8,128)(2,1)}, u32[]{:S(2)}) copy-start(bf16[1,512,2048]{2,1,0:T(8,128)(2,1)} %param.3) | copy-start | bytes 6291460
Sparse Core Ops, SparseCore 0:
  28.5 39.3 all-gather.6
  69.7 36.5 all-gather.4
  126.9 156.0 reduce-scatter.1
  285.2 121.0 all-reduce.1
where the time goes:
time: 421 us; the launch traced here: 420 us
  waiting for transfers between devices  311 us (74%)
  matrix products  63.7 us (15%)
  local copies, waits for them, and re-layouts  19.4 us (5%)
  between operations  14 us (3%)
  other arithmetic  11.8 us (3%)
    reduce_scatter x1, waiting for transfers between devices, body(): lax.psum_scatter(lax.dot_general(local_x, qkv_grad, (((0,), (0,)), ((), (...  156 us
    psum x1, waiting for transfers between devices, body(): summed = lax.psum(partial_rows, 'batch')  103 us
    all_gather x1, waiting for transfers between devices, body(): lax.all_gather(kv_local[None], 'seq', axis=0, tiled=True)  31.1 us
    all_gather x1, waiting for transfers between devices, body(): lax.all_gather(grad_local[None], 'seq', axis=0, tiled=True)  20.4 us
    dot_general x1, matrix products, body(): lax.dot_general(local_x, qkv_grad, (((0,), (0,)), ((), ())), preferred_el...  15.2 us
    dot_general x1, matrix products, body(): lax.dot_general(qkv_grad, w_qkv, (((1,), (1,)), ((), ())), preferred_elem...  13.6 us
    unnamed x44, local copies, waits for them, and re-layouts  12 us
    dot_general x1, matrix products, body(): jnp.dot(local_x, w_qkv, preferred_element_type=jnp.float32)  9.63 us
  transfers between devices with their start and end apart: 4, of which 4 were waited for; matrix products, arithmetic and copies ran while one was open for 11% of the time, Pallas kernels for 0%

commit v1 on v0

--- a/solution.py
+++ b/solution.py
@@ -1,6 +1,10 @@
+import functools
+
 import jax
 import jax.numpy as jnp
 from jax import lax
+from jax.experimental import pallas as pl
+from jax.experimental.pallas import tpu as pltpu
 from jax.sharding import PartitionSpec as P
 
 HEADS = 8
@@ -18,6 +22,243 @@
         return incoming[None] + jnp.concatenate([totals[1:], zero_block], 0)
     totals = jnp.cumsum(block_states, axis=0)
     return incoming[None] + jnp.concatenate([zero_block, totals[:-1]], 0)
+
+
+COLS = 256
+MESH = pl.DeviceIdType.MESH
+
+
+def bits_of(count):
+    bits = count.bit_length() - 1
+    assert count == 1 << bits
+    return bits
+
+
+def carries(kv_local, grad_local, seq_count):
+    bits = bits_of(seq_count)
+    rank = lax.axis_index("seq")
+    half = kv_local.shape[0] // 2
+
+    def swap(value, bit):
+        return lax.ppermute(value, "seq", [(i, i ^ (1 << bit)) for i in range(seq_count)])
+
+    def sides(value, bit):
+        upper = ((rank >> bit) & 1) == 1
+        return jnp.stack([jnp.where(upper, value[0], 0.0), jnp.where(upper, 0.0, value[1])])
+
+    own = jnp.stack([kv_local, grad_local])
+    other = swap(own, 0)
+    near = sides(other, 0)
+    total = lax.dynamic_slice_in_dim(own + other, (rank & 1) * half, half, 1)
+    far = jnp.zeros_like(total)
+    for bit in range(1, bits):
+        other = swap(total, bit)
+        far = far + sides(other, bit)
+        total = total + other
+    mate = swap(far, 0)
+    low = (rank & 1) == 0
+    joined = jnp.concatenate([jnp.where(low, far, mate), jnp.where(low, mate, far)], 1)
+    result = near + joined
+    return result[0], result[1]
+
+
+def orders(bits):
+    rest = list(range(1, bits))
+    cut = len(rest) // 2
+    return [[0] + rest, [0] + rest[cut:] + rest[:cut]]
+
+
+def reduce_kernel(seq_count, batch_count, x_ref, g_ref, o_ref, mine, first, *rest):
+    bits = bits_of(seq_count)
+    lands = [first] + list(rest[: bits - 1])
+    from_outer, from_inner, send_sem, recv_sem, z_send, z_recv = rest[bits - 1 :]
+    chunks = mine.shape[0]
+    half = mine.shape[1]
+    own_rows = o_ref.shape[0]
+    places = seq_count // 2
+    order = orders(bits)
+    rank = lax.axis_index("seq")
+    plane = lax.axis_index("batch")
+    middle = batch_count // 2
+    low_side = plane < middle
+    depth = jnp.where(low_side, middle - 1 - plane, plane - middle)
+    has_outer = jnp.where(low_side, plane > 0, plane < batch_count - 1)
+    is_inner = depth == 0
+    inner = jnp.where(low_side, plane + 1, plane - 1)
+    outer = jnp.where(low_side, plane - 1, plane + 1)
+
+    barrier = pltpu.get_barrier_semaphore()
+    for bit in range(bits):
+        pl.semaphore_signal(barrier, inc=1, device_id={"seq": rank ^ (1 << bit)}, device_id_type=MESH)
+    pl.semaphore_signal(barrier, inc=1, device_id={"batch": inner}, device_id_type=MESH)
+
+    @pl.when(has_outer)
+    def _():
+        pl.semaphore_signal(barrier, inc=1, device_id={"batch": outer}, device_id_type=MESH)
+
+    pl.semaphore_wait(barrier, bits + 1 + has_outer.astype(jnp.int32))
+
+    def step_copy(chunk, step):
+        size = half >> step
+        source = mine.at[chunk] if step == 0 else first.at[chunk, pl.ds(size, size)]
+        return pltpu.make_async_remote_copy(
+            src_ref=source,
+            dst_ref=lands[step].at[chunk],
+            send_sem=send_sem.at[step, chunk],
+            recv_sem=recv_sem.at[step, chunk],
+            device_id={"seq": rank ^ (1 << order[chunk % 2][step])},
+            device_id_type=MESH,
+        )
+
+    def inward(chunk, target):
+        return pltpu.make_async_remote_copy(
+            src_ref=first.at[chunk, pl.ds(0, own_rows)],
+            dst_ref=target.at[chunk],
+            send_sem=z_send.at[0, chunk],
+            recv_sem=z_recv.at[0 if target is from_outer else 1, chunk],
+            device_id={"batch": inner},
+            device_id_type=MESH,
+        )
+
+    def outward(chunk):
+        return pltpu.make_async_remote_copy(
+            src_ref=from_inner.at[chunk],
+            dst_ref=from_inner.at[chunk],
+            send_sem=z_send.at[1, chunk],
+            recv_sem=z_recv.at[1, chunk],
+            device_id={"batch": outer},
+            device_id_type=MESH,
+        )
+
+    def product(chunk, place):
+        owner = rank ^ sum(
+            (place // (1 << (bits - 1 - k)) % 2) * (1 << bit) for k, bit in enumerate(order[chunk % 2])
+        )
+        return jnp.dot(
+            x_ref[pl.ds(pl.multiple_of(owner * own_rows, own_rows), own_rows), :],
+            g_ref[:, chunk * COLS : (chunk + 1) * COLS],
+            preferred_element_type=jnp.float32,
+        )
+
+    def open_chunk(chunk):
+        @pl.loop(0, places)
+        def _(place):
+            row = pl.multiple_of(place * own_rows, own_rows)
+            mine[chunk, pl.ds(row, own_rows), :] = product(chunk, places + place)
+
+        step_copy(chunk, 0).start()
+
+    def enter(chunk):
+        step_copy(chunk, 0).wait_recv()
+
+        @pl.loop(0, places)
+        def _(place):
+            row = pl.multiple_of(place * own_rows, own_rows)
+            first[chunk, pl.ds(row, own_rows), :] += product(chunk, place)
+
+        if bits > 1:
+            step_copy(chunk, 1).start()
+
+    def halve(chunk, step):
+        step_copy(chunk, step).wait_recv()
+        size = half >> step
+        first[chunk, pl.ds(0, size), :] += lands[step][chunk]
+        if step + 1 < bits:
+            step_copy(chunk, step + 1).start()
+
+    def leave(chunk):
+        @pl.when(jnp.logical_not(has_outer) & jnp.logical_not(is_inner))
+        def _():
+            inward(chunk, from_outer).start()
+
+        @pl.when(jnp.logical_not(has_outer) & is_inner)
+        def _():
+            inward(chunk, from_inner).start()
+
+    def gather(chunk):
+        @pl.when(has_outer)
+        def _():
+            inward(chunk, from_outer).wait_recv()
+            first[chunk, pl.ds(0, own_rows), :] += from_outer[chunk]
+
+        @pl.when(has_outer & is_inner)
+        def _():
+            inward(chunk, from_inner).start()
+
+        @pl.when(has_outer & jnp.logical_not(is_inner))
+        def _():
+            inward(chunk, from_outer).start()
+
+    def close(chunk):
+        inward(chunk, from_inner).wait_recv()
+
+        @pl.when(is_inner)
+        def _():
+            from_inner[chunk] += first[chunk, pl.ds(0, own_rows), :]
+
+        @pl.when(has_outer)
+        def _():
+            outward(chunk).start()
+
+        o_ref[:, chunk * COLS : (chunk + 1) * COLS] = from_inner[chunk]
+
+    stages = [enter]
+    stages += [functools.partial(halve, step=step) for step in range(1, bits)]
+    stages += [leave, gather, close]
+    lag = list(range(bits)) + [bits - 1, bits, bits + 1]
+    pairs = chunks // 2
+    ahead = 2
+    for pair in range(min(ahead, pairs)):
+        open_chunk(2 * pair)
+        open_chunk(2 * pair + 1)
+    for slot in range(pairs + lag[-1]):
+        for stage, late in zip(stages, lag):
+            pair = slot - late
+            if 0 <= pair < pairs:
+                stage(2 * pair)
+                stage(2 * pair + 1)
+            if stage is enter and slot + ahead < pairs:
+                open_chunk(2 * (slot + ahead))
+                open_chunk(2 * (slot + ahead) + 1)
+    for chunk in range(chunks):
+        for step in range(bits):
+            step_copy(chunk, step).wait_send()
+        inward(chunk, from_inner).wait_send()
+
+        @pl.when(has_outer)
+        def _():
+            outward(chunk).wait_send()
+
+
+def reduced_rows(local_x, qkv_grad, seq_count, batch_count):
+    bits = bits_of(seq_count)
+    positions, width = local_x.shape
+    columns = qkv_grad.shape[1]
+    chunks = columns // COLS
+    half = width // 2
+    own_rows = width // seq_count
+    flops = 2 * positions * width * columns
+    return pl.pallas_call(
+        functools.partial(reduce_kernel, seq_count, batch_count),
+        out_shape=jax.ShapeDtypeStruct((own_rows, columns), jnp.float32),
+        in_specs=[pl.BlockSpec(memory_space=pltpu.VMEM)] * 2,
+        out_specs=pl.BlockSpec(memory_space=pltpu.VMEM),
+        scratch_shapes=[
+            pltpu.VMEM((chunks, half, COLS), jnp.float32),
+            pltpu.VMEM((chunks, half, COLS), jnp.float32),
+            *[pltpu.VMEM((chunks, half >> step, COLS), jnp.float32) for step in range(1, bits)],
+            pltpu.VMEM((chunks, own_rows, COLS), jnp.float32),
+            pltpu.VMEM((chunks, own_rows, COLS), jnp.float32),
+            pltpu.SemaphoreType.DMA((bits, chunks)),
+            pltpu.SemaphoreType.DMA((bits, chunks)),
+            pltpu.SemaphoreType.DMA((2, chunks)),
+            pltpu.SemaphoreType.DMA((2, chunks)),
+        ],
+        compiler_params=pltpu.CompilerParams(
+            collective_id=0, has_side_effects=True, vmem_limit_bytes=60 * 1024 * 1024
+        ),
+        cost_estimate=pl.CostEstimate(flops=flops, bytes_accessed=4 * width * columns, transcendentals=0),
+    )(local_x.T, qkv_grad)
 
 
 def body(tokens, w_qkv, cotangent):
@@ -43,14 +284,7 @@
     )
     kv_local = jnp.sum(kv_blocks, 0)
     grad_local = jnp.sum(grad_blocks, 0)
-    kv_all, grad_all = (
-        lax.all_gather(kv_local[None], "seq", axis=0, tiled=True),
-        lax.all_gather(grad_local[None], "seq", axis=0, tiled=True),
-    )
-    rank_list = jnp.arange(seq_count, dtype=jnp.int32)
-    my_rank = lax.axis_index("seq")
-    kv_in = jnp.sum(jnp.where((rank_list < my_rank)[:, None, None, None], kv_all, 0.0), 0)
-    grad_in = jnp.sum(jnp.where((rank_list > my_rank)[:, None, None, None], grad_all, 0.0), 0)
+    kv_in, grad_in = carries(kv_local, grad_local, seq_count)
     kv_before = running_states(kv_blocks, kv_in, False)
     grad_after = running_states(grad_blocks, grad_in, True)
     causal = jnp.arange(BLK)[:, None] >= jnp.arange(BLK)[None, :]
@@ -97,15 +331,7 @@
         qkv_grad, w_qkv, (((1,), (1,)), ((), ())), preferred_element_type=jnp.float32
     )
     token_grad = token_grad.astype(jnp.bfloat16)[None]
-    partial_rows = lax.psum_scatter(
-        lax.dot_general(
-            local_x, qkv_grad, (((0,), (0,)), ((), ())), preferred_element_type=jnp.float32
-        ),
-        "seq",
-        scatter_dimension=0,
-        tiled=True,
-    )
-    summed = lax.psum(partial_rows, "batch")
+    summed = reduced_rows(local_x, qkv_grad, seq_count, batch_count)
     grad_scale = 1.0 / jnp.sqrt(jnp.float32(batch_count * seq_count * row_count))
     weight_grad = summed * grad_scale
     return (attended.reshape(row_count, width).astype(jnp.bfloat16)[None], token_grad, weight_grad)

time: 421 us -> 267 us (0.63)
  waiting for transfers between devices: 311 us -> 11.4 us
  Pallas kernels: 0 us -> 158 us
  between operations: 14 us -> 0.89 us
  matrix products: 63.7 us -> 52 us
  starting transfers between devices: 0.34 us -> 4.88 us
  local copies, waits for them, and re-layouts: 19.4 us -> 23.7 us
    pallas_call x0 -> x1, Pallas kernels: none -> 158 us  [reduced_rows(): pl.pallas_call(functools.partial(reduce_kernel, seq_count, batch_count),...]
    reduce_scatter x1 -> x0, waiting for transfers between devices: 156 us -> none  [body(): lax.psum_scatter(lax.dot_general(local_x, qkv_grad, (((0,), (0,)), ((), (...]
    psum x1 -> x0, waiting for transfers between devices: 103 us -> none  [body(): summed = lax.psum(partial_rows, 'batch')]
    all_gather x2 -> x0, waiting for transfers between devices: 51.5 us -> none  [the longest x1 31.1 us: body(): lax.all_gather(kv_local[None], 'seq', axis=0, tiled=True)]
    dot_general x1 -> x0, matrix products: 15.2 us -> none  [body(): lax.dot_general(local_x, qkv_grad, (((0,), (0,)), ((), ())), preferred_el...]
    ppermute x0 -> x4, waiting for transfers between devices: none -> 11.4 us  [swap(): lax.ppermute(value, 'seq', [(i, i ^ 1 << bit) for i in range(seq_count)])]
    reduce_sum x2 -> x0, other arithmetic: 5.8 us -> none  [the longest x1 2.9 us: body(): jnp.sum(jnp.where((rank_list < my_rank)[:, None, None, None], kv_all, 0.0...]
    reshape x1 -> x4, local copies, waits for them, and re-layouts: 2.29 us -> 7.49 us  [the longest x1 2.28 us: body(): value_grad.reshape(row_count, width)]
  transfers between devices with their start and end apart: 4 -> 4, of which waited for: 4 -> 2; matrix products, arithmetic and copies ran while one was open for 11% -> 9% of each run, Pallas kernels for 0% -> 0%
where the time goes in v1:
time: 267 us
  Pallas kernels  158 us (59%)
  matrix products  52 us (19%)
  local copies, waits for them, and re-layouts  23.7 us (9%)
  other arithmetic  15.8 us (6%)
  waiting for transfers between devices  11.4 us (4%)
  starting transfers between devices  4.88 us (2%)
    pallas_call x1, Pallas kernels, reduced_rows(): pl.pallas_call(functools.partial(reduce_kernel, seq_count, batch_count),...  158 us
    unnamed x37, local copies, waits for them, and re-layouts  13 us
    ppermute x4, waiting for transfers between devices, swap(): lax.ppermute(value, 'seq', [(i, i ^ 1 << bit) for i in range(seq_count)])  11.4 us
    dot_general x1, matrix products, body(): lax.dot_general(qkv_grad, w_qkv, (((1,), (1,)), ((), ())), preferred_elem...  11.1 us
    dot_general x1, matrix products, body(): jnp.dot(local_x, w_qkv, preferred_element_type=jnp.float32)  10.3 us
  transfers between devices with their start and end apart: 4, of which 2 were waited for; matrix products, arithmetic and copies ran while one was open for 9% of the time, Pallas kernels for 0%

profile of v1, /device:TPU:0, one launch (start us, length us, event | category | flops | bytes accessed | tf_op | source)
XLA Modules:
  0.0 266.7 jit_solution(12084871571444526296)
XLA Ops:
  0.6 10.3 %convolution_convert_fusion = bf16[512,3072]{1,0:T(8,128)(2,1)S(1)} fusion(bf16[2048,3072]{1,0:T(8,128)(2,1)} %param.4, bf16[1,512,2048]{2,1,0:T(8,128)(2,1)} %param.3), kind=kOutput, calls=%fused_computation.2 | convolution fusion | flops 6444023808 | bytes 17825792 | tf_op jit(solution)/shard_map/dot_general | solution.py:271
  10.9 2.7 slice_bitcast_fusion.2
  13.6 1.5 copy.42
  15.1 1.5 copy.13
  16.5 2.6 copy.34
  19.1 0.3 copy.41
  19.4 0.7 copy.10
  20.1 1.9 multiply_convert_fusion
  21.9 1.7 convolution_bitcast_fusion
  23.6 0.0 copy-start.4
  23.6 0.5 convolution_bitcast_fusion.1
  24.1 0.4 copy-done.4
  24.4 1.2 pad_maximum_fusion.1
  25.6 0.0 copy-done.7
  25.6 0.5 collective-permute-start
  26.1 0.1 iota_compare_fusion
  26.2 2.9 %select_convert_fusion.1 = bf16[8,512,512]{2,1,0:T(8,128)(2,1)S(1)} fusion(pred[512,512]{1,0:T(8,128)(4,1)S(1)} %iota_compare_fusion, bf16[64,8,8,128]{3,2,1,0:T(8,128)(2,1)} %get-tuple-element.8, bf16[64,8,8,128]{3,2,1,0:T(8,128)(2,1)} %get-tuple-element.7), kind=kOutput, calls=%fused_computation.1 | convolution fusion | flops 541065216 | bytes 6553600 | tf_op jit(solution)/shard_map/nihd,njhd->nhij/dot_general | solution.py:293
  29.0 0.0 copy-start.1
  29.0 0.0 copy-start.5
  29.1 0.0 copy-start.8
  29.1 2.9 %fusion.7 = f32[8,128,512]{2,1,0:T(8,128)} fusion(bf16[8,512,512]{2,1,0:T(8,128)(2,1)S(1)} %select_convert_fusion.1, bf16[64,8,8,128]{3,2,1,0:T(8,128)(2,1)S(1)} %get-tuple-element.10), kind=kOutput, calls=%fused_computation.23 | convolution fusion | flops 536870912 | bytes 7340032 | tf_op jit(solution)/shard_map/nhij,njhd->nihd/dot_general | solution.py:305
  32.0 0.0 copy-done.1
  32.0 0.0 collective-permute-done
  32.0 0.0 copy-done.5
  32.0 0.0 copy-done.8
  32.0 1.9 fusion.21
  33.9 2.5 collective-permute-start.1
  36.4 3.4 %select_convert_fusion = bf16[8,512,512]{2,1,0:T(8,128)(2,1)} fusion(pred[512,512]{1,0:T(8,128)(4,1)S(1)} %iota_compare_fusion, bf16[512,8,128]{0,2,1:T(8,128)(2,1)S(1)} %multiply_convert_fusion, bf16[64,8,8,128]{3,2,1,0:T(8,128)(2,1)S(1)} %get-tuple-element.10), kind=kOutput, calls=%fused_computation | convolution fusion | flops 541065216 | bytes 6553600 | tf_op jit(solution)/shard_map/nihd,njhd->nhij/dot_general | solution.py:298
  39.8 3.9 %copy.6 = bf16[1,512,2048]{1,2,0:T(8,128)(2,1)} copy(bf16[1,512,2048]{2,1,0:T(8,128)(2,1)} %param.3) | data formatting | bytes 4194304 | tf_op args[0]
  43.7 3.0 %fusion.24 = f32[8,128,512]{2,1,0:T(8,128)S(1)} fusion(bf16[512,8,128]{0,2,1:T(8,128)(2,1)S(1)} %multiply_convert_fusion, bf16[8,512,512]{2,1,0:T(8,128)(2,1)} %copy-done.1), kind=kOutput, calls=%fused_computation.59 | convolution fusion | flops 536870912 | bytes 7340032 | tf_op jit(solution)/shard_map/nhij,nihe->njhe/dot_general | solution.py:318
  46.8 0.0 copy-start.2
  46.8 2.5 collective-permute-done.1
  49.3 0.0 copy-done.6
  49.3 0.0 copy-done.9
  49.3 1.3 fusion.39
  50.6 1.8 collective-permute-start.2
  52.4 0.0 copy-done.2
  52.4 2.0 fusion.23
  54.5 1.1 slice_select_fusion.5
  55.5 8.9 %collective-permute-done.2 = f32[2,4,128,128]{3,2,1,0:T(8,128)S(1)} collective-permute-done((f32[2,4,128,128]{3,2,1,0:T(8,128)S(1)}, f32[2,4,128,128]{3,2,1,0:T(8,128)S(1)}, u32[]{:S(2)}, u32[]{:S(2)}) %collective-permute-start.2) | collective-permute-done | bytes 524320 | tf_op jit(solution)/shard_map/ppermute | solution.py:43
  64.5 0.1 maximum_add_fusion.1
  64.5 0.1 collective-permute-start.3
  64.6 2.8 %fusion.22 = f32[8,128,512]{2,1,0:T(8,128)} fusion(bf16[512,8,128]{0,2,1:T(8,128)(2,1)S(1)} %copy.10, bf16[8,512,512]{2,1,0:T(8,128)(2,1)S(1)} %copy-done), kind=kOutput, calls=%fused_computation.57 | convolution fusion | flops 536870912 | bytes 7340032 | tf_op jit(solution)/shard_map/nhij,njhd->nihd/dot_general | solution.py:310
  67.4 1.3 slice_select_fusion.1
  68.7 0.0 collective-permute-done.3
  68.7 0.1 broadcast_select_fusion.1
  68.8 0.1 maximum_add_fusion
  69.0 1.0 copy-done.15
  69.9 2.0 add_convert_fusion
  72.0 2.3 copy.37
  74.3 3.6 %add_convert_fusion.1 = bf16[8,128,512]{2,1,0:T(8,128)(2,1)} fusion(f32[8,128,512]{2,1,0:T(8,128)} %fusion.23, bf16[64,8,8,128]{3,2,1,0:T(8,128)(2,1)S(1)} %get-tuple-element.10, f32[2,8,128,128]{3,2,1,0:T(8,128)S(1)} %maximum_add_fusion), kind=kOutput, calls=%fused_computation.10 | convolution fusion | flops 806354944 | bytes 4718592 | tf_op jit(solution)/shard_map/njhe,nhde->njhd/dot_general | solution.py:317
  77.9 2.3 copy.36
  80.2 3.7 %add_convert_fusion.2 = bf16[8,128,512]{2,1,0:T(8,128)(2,1)} fusion(f32[8,128,512]{2,1,0:T(8,128)} %fusion.22, bf16[512,8,128]{0,2,1:T(8,128)(2,1)S(1)} %multiply_convert_fusion, f32[2,8,128,128]{3,2,1,0:T(8,128)S(1)} %maximum_add_fusion), kind=kOutput, calls=%fused_computation.11 | convolution fusion | flops 806354944 | bytes 4718592 | tf_op jit(solution)/shard_map/nihe,nhde->nihd/dot_general | solution.py:313
  83.8 1.5 copy.35
  85.3 1.0 copy-done.13
  86.3 0.0 copy-done.10
  86.3 11.1 %fusion = bf16[1,512,2048]{2,1,0:T(8,128)(2,1)} fusion(bf16[2048,3072]{1,0:T(8,128)(2,1)} %param.4, bf16[512,1024]{1,0:T(8,128)(2,1)S(1)} %copy-done.10, bf16[512,1024]{1,0:T(8,128)(2,1)} %copy.36, bf16[512,1024]{1,0:T(8,128)(2,1)S(1)} %copy.35), kind=kOutput, calls=%fused_computation.5 | convolution fusion | flops 6452936704 | bytes 17825792 | tf_op jit(solution)/shard_map/dot_general | solution.py:330
  97.4 0.0 copy-done.12
  97.4 0.0 copy-start.14
  97.4 3.0 %pad_maximum_fusion.g_ref = bf16[512,3072]{1,0:T(8,128)(2,1)} fusion(bf16[512,1024]{1,0:T(8,128)(2,1)S(1)} %copy-done.11, bf16[512,1024]{1,0:T(8,128)(2,1)S(1)} %copy-done.12, bf16[512,1024]{1,0:T(8,128)(2,1)} %copy-done.13), kind=kLoop, calls=%fused_computation.3 | loop fusion | flops 9437184 | bytes 6291456 | tf_op jit(solution)/shard_map/concatenate | solution.py:322
  100.4 2.1 fusion.2
  102.5 2.3 copy.28
  104.7 158.0 %shard_map.58 = f32[256,3072]{1,0:T(8,128)} custom-call(bf16[2048,512]{1,0:T(8,128)(2,1)} %bitcast.95, bf16[512,3072]{1,0:T(8,128)(2,1)} %pad_maximum_fusion.g_ref), custom_call_target="tpu_custom_call" | custom-call | flops 6442450944 | bytes 25165824 | tf_op jit(solution)/shard_map/pallas_call | solution.py:241
  262.8 3.9 %broadcast_multiply_fusion = f32[256,3072]{1,0:T(8,128)} fusion(f32[256,3072]{1,0:T(8,128)} %shard_map.58), kind=kLoop, calls=%fused_computation.13 | loop fusion | flops 786432 | bytes 6291456 | tf_op jit(solution)/shard_map/mul | solution.py:336
  (16 shorter events, 0.1 us)
Async XLA Ops:
  23.6 0.8 copy-start.4
  24.4 1.2 copy-start.7
  25.6 6.4 %collective-permute-start = (f32[2,8,128,128]{3,2,1,0:T(8,128)}, f32[2,8,128,128]{3,2,1,0:T(8,128)}, u32[]{:S(2)}, u32[]{:S(2)}) collective-permute-start(f32[2,8,128,128]{3,2,1,0:T(8,128)} %pad_maximum_fusion.1), channel_id=1, source_target_pairs={{0,4},{4,0},{8,12},{12,8},{16,20},{20,16},{24,28},{28,24},{1,5},{5... | collective-permute-start | bytes 3145736 | tf_op jit(solution)/shard_map/ppermute | solution.py:43
  29.0 2.9 %copy-start.1 = (bf16[8,512,512]{2,1,0:T(8,128)(2,1)}, bf16[8,512,512]{2,1,0:T(8,128)(2,1)S(1)}, u32[]{:S(2)}) copy-start(bf16[8,512,512]{2,1,0:T(8,128)(2,1)S(1)} %select_convert_fusion.1) | copy-start | bytes 12582916
  29.0 2.9 %copy-start.5 = (f32[1,8,128,128]{3,2,1,0:T(8,128)S(1)}, f32[1,8,128,128]{3,2,1,0:T(8,128)}, u32[]{:S(2)}) copy-start(f32[1,8,128,128]{3,2,1,0:T(8,128)} %copy-done.4) | copy-start | bytes 1572868
  29.1 2.9 %copy-start.8 = (f32[1,8,128,128]{3,2,1,0:T(8,128)S(1)}, f32[1,8,128,128]{3,2,1,0:T(8,128)}, u32[]{:S(2)}) copy-start(f32[1,8,128,128]{3,2,1,0:T(8,128)} %copy-done.7) | copy-start | bytes 1572868
  33.9 15.4 %collective-permute-start.1 = (f32[2,4,128,128]{3,2,1,0:T(8,128)}, f32[2,4,128,128]{3,2,1,0:T(8,128)}, u32[]{:S(2)}, u32[]{:S(2)}) collective-permute-start(f32[2,4,128,128]{3,2,1,0:T(8,128)} %fusion.21), channel_id=1, source_target_pairs={{0,8},{4,12},{8,0},{12,4},{16,24},{20,28},{24,16},{28,20},{1,9},{5... | collective-permute-start | bytes 1572872 | tf_op jit(solution)/shard_map/ppermute | solution.py:43
  43.7 5.6 %copy-start.6 = (f32[1,8,128,128]{3,2,1,0:T(8,128)S(1)}, f32[1,8,128,128]{3,2,1,0:T(8,128)}, u32[]{:S(2)}) copy-start(f32[1,8,128,128]{3,2,1,0:T(8,128)} %copy-done.4) | copy-start | bytes 1572868
  43.7 5.6 %copy-start.9 = (f32[1,8,128,128]{3,2,1,0:T(8,128)S(1)}, f32[1,8,128,128]{3,2,1,0:T(8,128)}, u32[]{:S(2)}) copy-start(f32[1,8,128,128]{3,2,1,0:T(8,128)} %copy-done.7) | copy-start | bytes 1572868
  43.7 8.7 %copy-start = (bf16[8,512,512]{2,1,0:T(8,128)(2,1)S(1)}, bf16[8,512,512]{2,1,0:T(8,128)(2,1)}, u32[]{:S(2)}) copy-start(bf16[8,512,512]{2,1,0:T(8,128)(2,1)} %select_convert_fusion) | copy-start | bytes 12582916
  46.8 5.7 %copy-start.2 = (bf16[512,8,128]{0,2,1:T(8,128)(2,1)S(1)}, bf16[512,8,128]{0,2,1:T(8,128)(2,1)}, u32[]{:S(2)}) copy-start(bf16[512,8,128]{0,2,1:T(8,128)(2,1)} %copy.13) | copy-start | bytes 3145732
  50.6 13.8 %collective-permute-start.2 = (f32[2,4,128,128]{3,2,1,0:T(8,128)S(1)}, f32[2,4,128,128]{3,2,1,0:T(8,128)S(1)}, u32[]{:S(2)}, u32[]{:S(2)}) collective-permute-start(f32[2,4,128,128]{3,2,1,0:T(8,128)S(1)} %fusion.39), channel_id=1, source_target_pairs={{0,16},{4,20},{8,24},{12,28},{16,0},{20,4},{24,8},{28,12},{1,17},{... | collective-permute-start | bytes 1572872 | tf_op jit(solution)/shard_map/ppermute | solution.py:43
  64.5 4.2 %collective-permute-start.3 = (f32[2,4,128,128]{3,2,1,0:T(8,128)S(1)}, f32[2,4,128,128]{3,2,1,0:T(8,128)S(1)}, u32[]{:S(2)}, u32[]{:S(2)}) collective-permute-start(f32[2,4,128,128]{3,2,1,0:T(8,128)S(1)} %maximum_add_fusion.1), channel_id=1, source_target_pairs={{0,4},{4,0},{8,12},{12,8},{16,20},{20,16},{24,28},{28,24},{1,5},{5... | collective-permute-start | bytes 1572872 | tf_op jit(solution)/shard_map/ppermute | solution.py:43
  68.7 1.2 copy-start.15
  80.2 6.2 %copy-start.10 = (bf16[512,1024]{1,0:T(8,128)(2,1)S(1)}, bf16[512,1024]{1,0:T(8,128)(2,1)}, u32[]{:S(2)}) copy-start(bf16[512,1024]{1,0:T(8,128)(2,1)} %copy.37) | copy-start | bytes 3145732
  85.3 1.0 copy-start.13
  86.3 11.1 %copy-start.11 = (bf16[512,1024]{1,0:T(8,128)(2,1)S(1)}, bf16[512,1024]{1,0:T(8,128)(2,1)}, u32[]{:S(2)}) copy-start(bf16[512,1024]{1,0:T(8,128)(2,1)} %copy.37) | copy-start | bytes 3145732
  86.3 11.1 %copy-start.12 = (bf16[512,1024]{1,0:T(8,128)(2,1)S(1)}, bf16[512,1024]{1,0:T(8,128)(2,1)}, u32[]{:S(2)}) copy-start(bf16[512,1024]{1,0:T(8,128)(2,1)} %copy.36) | copy-start | bytes 3145732
  97.4 3.0 %copy-start.3 = (f32[8,128,512]{2,1,0:T(8,128)S(1)}, f32[8,128,512]{2,1,0:T(8,128)}, u32[]{:S(2)}) copy-start(f32[8,128,512]{2,1,0:T(8,128)} %fusion.7) | copy-start | bytes 6291460
  97.4 3.0 %copy-start.14 = (bf16[64,8,8,128]{3,2,1,0:T(8,128)(2,1)S(1)}, bf16[64,8,8,128]{3,2,1,0:T(8,128)(2,1)}, u32[]{:S(2)}) copy-start(bf16[64,8,8,128]{3,2,1,0:T(8,128)(2,1)} %get-tuple-element.7) | copy-start | bytes 3145732

commit v2 on v1

v2 whole, which is shorter than its diff:
```python
import functools

import jax
import jax.numpy as jnp
from jax import lax
from jax.experimental import pallas as pl
from jax.experimental.pallas import tpu as pltpu
from jax.sharding import PartitionSpec as P

HEADS = 8
DH = 128
BLK = 512


COLS = 128
MESH = pl.DeviceIdType.MESH


def bits_of(count):
    bits = count.bit_length() - 1
    assert count == 1 << bits
    return bits


def carries(own, seq_count):
    bits = bits_of(seq_count)
    rank = lax.axis_index("seq")
    half = own.shape[1] // 2

    def swap(value, bit):
        return lax.ppermute(value, "seq", [(i, i ^ (1 << bit)) for i in range(seq_count)])

    def sides(value, bit):
        upper = ((rank >> bit) & 1) == 1
        return jnp.stack([jnp.where(upper, value[0], 0.0), jnp.where(upper, 0.0, value[1])])

    other = swap(own, 0)
    near = sides(other, 0)
    total = lax.dynamic_slice_in_dim(own + other, (rank & 1) * half, half, 1)
    far = jnp.zeros_like(total)
    for bit in range(1, bits):
        other = swap(total, bit)
        far = far + sides(other, bit)
        total = total + other
    mate = swap(far, 0)
    low = (rank & 1) == 0
    joined = jnp.concatenate([jnp.where(low, far, mate), jnp.where(low, mate, far)], 1)
    result = near + joined
    return result[0], result[1]


def orders(bits):
    rest = list(range(1, bits))
    cut = len(rest) // 2
    return [[0] + rest, [0] + rest[cut:] + rest[:cut]]


def reduce_kernel(seq_count, batch_count, x_ref, g_ref, w_hbm, o_ref, t_ref, w_tiles, w_sem, mine, first, *rest):
    bits = bits_of(seq_count)
    lands = [first] + list(rest[: bits - 1])
    from_outer, from_inner, send_sem, recv_sem, z_send, z_recv = rest[bits - 1 :]
    chunks = mine.shape[0]
    half = mine.shape[1]
    own_rows = o_ref.shape[0]
    places = seq_count // 2
    order = orders(bits)
    rank = lax.axis_index("seq")
    plane = lax.axis_index("batch")
    middle = batch_count // 2
    low_side = plane < middle
    depth = jnp.where(low_side, middle - 1 - plane, plane - middle)
    has_outer = jnp.where(low_side, plane > 0, plane < batch_count - 1)
    is_inner = depth == 0
    inner = jnp.where(low_side, plane + 1, plane - 1)
    outer = jnp.where(low_side, plane - 1, plane + 1)

    barrier = pltpu.get_barrier_semaphore()
    for bit in range(bits):
        pl.semaphore_signal(barrier, inc=1, device_id={"seq": rank ^ (1 << bit)}, device_id_type=MESH)
    pl.semaphore_signal(barrier, inc=1, device_id={"batch": inner}, device_id_type=MESH)

    @pl.when(has_outer)
    def _():
        pl.semaphore_signal(barrier, inc=1, device_id={"batch": outer}, device_id_type=MESH)

    pl.semaphore_wait(barrier, bits + 1 + has_outer.astype(jnp.int32))

    def step_copy(chunk, step):
        size = half >> step
        source = mine.at[chunk] if step == 0 else first.at[chunk, pl.ds(size, size)]
        return pltpu.make_async_remote_copy(
            src_ref=source,
            dst_ref=lands[step].at[chunk],
            send_sem=send_sem.at[step, chunk],
            recv_sem=recv_sem.at[step, chunk],
            device_id={"seq": rank ^ (1 << order[chunk % 2][step])},
            device_id_type=MESH,
        )

    def inward(chunk, target):
        return pltpu.make_async_remote_copy(
            src_ref=first.at[chunk, pl.ds(0, own_rows)],
            dst_ref=target.at[chunk],
            send_sem=z_send.at[0, chunk],
            recv_sem=z_recv.at[0 if target is from_outer else 1, chunk],
            device_id={"batch": inner},
            device_id_type=MESH,
        )

    def outward(chunk):
        return pltpu.make_async_remote_copy(
            src_ref=from_inner.at[chunk],
            dst_ref=from_inner.at[chunk],
            send_sem=z_send.at[1, chunk],
            recv_sem=z_recv.at[1, chunk],
            device_id={"batch": outer},
            device_id_type=MESH,
        )

    def spots(owner_xor):
        return [
            sum((owner_xor // (1 << bit) % 2) * (1 << (bits - 1 - k)) for k, bit in enumerate(way) if k)
            for way in order
        ]

    def product(pair, owner_xor):
        owner = rank ^ owner_xor
        return jnp.dot(
            x_ref[pl.ds(pl.multiple_of(owner * own_rows, own_rows), own_rows), :],
            g_ref[:, pair * 2 * COLS : (pair + 1) * 2 * COLS],
            preferred_element_type=jnp.float32,
        )

    def open_pair(pair):
        @pl.loop(0, places)
        def _(index):
            value = product(pair, 2 * index + 1)
            for side, spot in enumerate(spots(2 * index + 1)):
                row = pl.multiple_of(spot * own_rows, own_rows)
                mine[2 * pair + side, pl.ds(row, own_rows), :] = value[:, side * COLS : (side + 1) * COLS]

        step_copy(2 * pair, 0).start()
        step_copy(2 * pair + 1, 0).start()

    def enter_pair(pair):
        step_copy(2 * pair, 0).wait_recv()
        step_copy(2 * pair + 1, 0).wait_recv()

        @pl.loop(0, places)
        def _(index):
            value = product(pair, 2 * index)
            for side, spot in enumerate(spots(2 * index)):
                row = pl.multiple_of(spot * own_rows, own_rows)
                first[2 * pair + side, pl.ds(row, own_rows), :] += value[:, side * COLS : (side + 1) * COLS]

        if bits > 1:
            step_copy(2 * pair, 1).start()
            step_copy(2 * pair + 1, 1).start()

    tile = w_tiles.shape[1]
    tiles = w_hbm.shape[0] // tile

    def w_copy(index):
        return pltpu.make_async_copy(
            w_hbm.at[pl.ds(index * tile, tile)], w_tiles.at[index % 2], w_sem.at[index % 2]
        )

    def token_tile(index):
        w_copy(index).wait()
        t_ref[:, index * tile : (index + 1) * tile] = lax.dot_general(
            g_ref[...], w_tiles[index % 2], (((1,), (1,)), ((), ())), preferred_element_type=jnp.float32
        ).astype(t_ref.dtype)
        if index + 2 < tiles:
            w_copy(index + 2).start()

    def halve(chunk, step):
        step_copy(chunk, step).wait_recv()
        size = half >> step
        first[chunk, pl.ds(0, size), :] += lands[step][chunk]
        if step + 1 < bits:
            step_copy(chunk, step + 1).start()

    def leave(chunk):
        @pl.when(jnp.logical_not(has_outer) & jnp.logical_not(is_inner))
        def _():
            inward(chunk, from_outer).start()

        @pl.when(jnp.logical_not(has_outer) & is_inner)
        def _():
            inward(chunk, from_inner).start()

    def gather(chunk):
        @pl.when(has_outer)
        def _():
            inward(chunk, from_outer).wait_recv()
            first[chunk, pl.ds(0, own_rows), :] += from_outer[chunk]

        @pl.when(has_outer & is_inner)
        def _():
            inward(chunk, from_inner).start()

        @pl.when(has_outer & jnp.logical_not(is_inner))
        def _():
            inward(chunk, from_outer).start()

    def close(chunk):
        inward(chunk, from_inner).wait_recv()

        @pl.when(is_inner)
        def _():
            from_inner[chunk] += first[chunk, pl.ds(0, own_rows), :]

        @pl.when(has_outer)
        def _():
            outward(chunk).start()

        o_ref[:, chunk * COLS : (chunk + 1) * COLS] = from_inner[chunk]

    stages = [functools.partial(halve, step=step) for step in range(1, bits)]
    stages += [leave, gather, close]
    lag = list(range(1, bits)) + [bits - 1, bits, bits + 1]
    pairs = chunks // 2
    ahead = 2
    for index in range(min(2, tiles)):
        w_copy(index).start()
    for pair in range(min(ahead, pairs)):
        open_pair(pair)
    for slot in range(pairs + lag[-1]):
        if slot < pairs:
            enter_pair(slot)
        if slot + ahead < pairs:
            open_pair(slot + ahead)
        for stage, late in zip(stages, lag):
            pair = slot - late
            if 0 <= pair < pairs:
                stage(2 * pair)
                stage(2 * pair + 1)
        if 1 <= slot <= tiles:
            token_tile(slot - 1)
    for index in range(pairs + lag[-1] - 1, tiles):
        token_tile(index)
    for chunk in range(chunks):
        for step in range(bits):
            step_copy(chunk, step).wait_send()
        inward(chunk, from_inner).wait_send()

        @pl.when(has_outer)
        def _():
            outward(chunk).wait_send()


def reduced_rows(local_x, qkv_grad, w_qkv, seq_count, batch_count):
    bits = bits_of(seq_count)
    positions, width = local_x.shape
    columns = qkv_grad.shape[1]
    chunks = columns // COLS
    half = width // 2
    own_rows = width // seq_count
    flops = 4 * positions * width * columns
    return pl.pallas_call(
        functools.partial(reduce_kernel, seq_count, batch_count),
        out_shape=(
            jax.ShapeDtypeStruct((own_rows, columns), jnp.float32),
            jax.ShapeDtypeStruct((positions, width), jnp.bfloat16),
        ),
        in_specs=[pl.BlockSpec(memory_space=pltpu.VMEM)] * 2 + [pl.BlockSpec(memory_space=pl.ANY)],
        out_specs=(pl.BlockSpec(memory_space=pltpu.VMEM), pl.BlockSpec(memory_space=pltpu.VMEM)),
        scratch_shapes=[
            pltpu.VMEM((2, 256, columns), jnp.bfloat16),
            pltpu.SemaphoreType.DMA((2,)),
            pltpu.VMEM((chunks, half, COLS), jnp.float32),
            pltpu.VMEM((chunks, half, COLS), jnp.float32),
            *[pltpu.VMEM((chunks, half >> step, COLS), jnp.float32) for step in range(1, bits)],
            pltpu.VMEM((chunks, own_rows, COLS), jnp.float32),
            pltpu.VMEM((chunks, own_rows, COLS), jnp.float32),
            pltpu.SemaphoreType.DMA((bits, chunks)),
            pltpu.SemaphoreType.DMA((bits, chunks)),
            pltpu.SemaphoreType.DMA((2, chunks)),
            pltpu.SemaphoreType.DMA((2, chunks)),
        ],
        compiler_params=pltpu.CompilerParams(
            collective_id=0, has_side_effects=True, vmem_limit_bytes=60 * 1024 * 1024
        ),
        cost_estimate=pl.CostEstimate(flops=flops, bytes_accessed=4 * width * columns, transcendentals=0),
    )(local_x.T, qkv_grad, w_qkv)


def dot(left, right, left_dim, right_dim):
    return lax.dot_general(
        left, right, (((left_dim,), (right_dim,)), ((), ())), preferred_element_type=jnp.float32
    )


def state_kernel(q_ref, k_ref, v_ref, c_ref, s_ref, g_ref, state_ref):
    grad = (c_ref[...].astype(jnp.float32) * s_ref[...]).astype(jnp.bfloat16)
    g_ref[...] = grad
    state_ref[0, 0] = dot(k_ref[...], v_ref[...], 0, 0)
    state_ref[1, 0] = dot(q_ref[...], grad, 0, 0)


def block_kernel(q_ref, k_ref, v_ref, g_ref, out_ref):
    query, key, value, grad = q_ref[...], k_ref[...], v_ref[...], g_ref[...]
    rows = lax.broadcasted_iota(jnp.int32, (BLK, BLK), 0)
    cols = lax.broadcasted_iota(jnp.int32, (BLK, BLK), 1)
    causal = rows >= cols
    scores = jnp.where(causal, dot(query, key, 1, 1), 0.0).astype(jnp.bfloat16)
    grad_scores = jnp.where(causal, dot(grad, value, 1, 1), 0.0).astype(jnp.bfloat16)
    out_ref[0] = dot(scores, value, 1, 0)
    out_ref[1] = dot(grad_scores, key, 1, 0)
    out_ref[2] = dot(grad_scores, query, 0, 0)
    out_ref[3] = dot(scores, grad, 0, 0)


def carry_kernel(q_ref, k_ref, v_ref, g_ref, s_ref, part_ref, kv_ref, gs_ref, a_ref, o_ref):
    head = pl.program_id(0)
    width = a_ref.shape[1] * pl.num_programs(0)

    def wide(left, state, state_dim):
        high = state.astype(jnp.bfloat16)
        rest = (state - high.astype(jnp.float32)).astype(jnp.bfloat16)
        return dot(left, high, 1, state_dim) + dot(left, rest, 1, state_dim)

    kv, grad_state = kv_ref[0], gs_ref[0]
    a_ref[...] = ((part_ref[0] + wide(q_ref[...], kv, 0)) * s_ref[...]).astype(a_ref.dtype)
    results = (
        part_ref[1] + wide(g_ref[...], kv, 1),
        part_ref[2] + wide(v_ref[...], grad_state, 1),
        part_ref[3] + wide(k_ref[...], grad_state, 0),
    )
    for index, result in enumerate(results):
        start = pl.multiple_of(index * width + head * DH, DH)
        o_ref[:, pl.ds(start, DH)] = result.astype(o_ref.dtype)


def body(tokens, w_qkv, cotangent):
    row_count = tokens.shape[1]
    width = w_qkv.shape[1] // 3
    assert row_count == BLK and width == HEADS * DH
    seq_count = lax.axis_size("seq")
    batch_count = lax.axis_size("batch")
    local_x = tokens[0]
    projected = jnp.dot(local_x, w_qkv, preferred_element_type=jnp.float32).astype(jnp.bfloat16)
    position = lax.axis_index("seq") * row_count + jnp.arange(row_count, dtype=jnp.int32)
    pos_scale = (DH ** (-0.5) / jnp.sqrt(position.astype(jnp.float32) + 1.0))[:, None]
    head_specs = [pl.BlockSpec((BLK, DH), lambda h, part=part: (0, part * HEADS + h)) for part in range(3)]
    own_spec = pl.BlockSpec((BLK, DH), lambda h: (0, h))
    scale_spec = pl.BlockSpec((BLK, 1), lambda h: (0, 0))
    part_spec = pl.BlockSpec((4, BLK, DH), lambda h: (0, 0, h))
    head_state = pl.BlockSpec((1, DH, DH), lambda h: (h, 0, 0))
    scaled_grad, states = pl.pallas_call(
        state_kernel,
        grid=(HEADS,),
        out_shape=(
            jax.ShapeDtypeStruct((row_count, width), jnp.bfloat16),
            jax.ShapeDtypeStruct((2, HEADS, DH, DH), jnp.float32),
        ),
        in_specs=head_specs + [own_spec, scale_spec],
        out_specs=(own_spec, pl.BlockSpec((2, 1, DH, DH), lambda h: (0, h, 0, 0))),
        cost_estimate=pl.CostEstimate(
            flops=4 * row_count * width * DH, bytes_accessed=10 * row_count * width, transcendentals=0
        ),
    )(projected, projected, projected, cotangent[0], pos_scale)
    parts = pl.pallas_call(
        block_kernel,
        grid=(HEADS,),
        out_shape=jax.ShapeDtypeStruct((4, row_count, width), jnp.float32),
        in_specs=head_specs + [own_spec],
        out_specs=part_spec,
        cost_estimate=pl.CostEstimate(
            flops=12 * row_count * width * BLK, bytes_accessed=24 * row_count * width, transcendentals=0
        ),
    )(projected, projected, projected, scaled_grad)
    kv_in, grad_in = carries(states, seq_count)
    attended, qkv_grad = pl.pallas_call(
        carry_kernel,
        grid=(HEADS,),
        out_shape=(
            jax.ShapeDtypeStruct((row_count, width), jnp.bfloat16),
            jax.ShapeDtypeStruct((row_count, 3 * width), jnp.bfloat16),
        ),
        in_specs=head_specs + [own_spec, scale_spec, part_spec, head_state, head_state],
        out_specs=(own_spec, pl.BlockSpec((BLK, 3 * width), lambda h: (0, 0))),
        cost_estimate=pl.CostEstimate(
            flops=16 * row_count * width * DH, bytes_accessed=32 * row_count * width, transcendentals=0
        ),
    )(projected, projected, projected, scaled_grad, pos_scale, parts, kv_in, grad_in)
    summed, token_grad = reduced_rows(local_x, qkv_grad, w_qkv, seq_count, batch_count)
    grad_scale = 1.0 / jnp.sqrt(jnp.float32(batch_count * seq_count * row_count))
    weight_grad = summed * grad_scale
    return attended[None], token_grad[None], weight_grad


def solution(mesh):
    return jax.shard_map(
        body,
        mesh=mesh,
        in_specs=(P("batch", "seq", None), P(), P("batch", "seq", None)),
        out_specs=(P("batch", "seq", None), P("batch", "seq", None), P("seq", None)),
        check_vma=False,
    )
```

time: 267 us -> 225 us (0.84)
  matrix products: 52 us -> 12.9 us
  local copies, waits for them, and re-layouts: 23.7 us -> 6.39 us
  Pallas kernels: 158 us -> 171 us
  waiting for transfers between devices: 11.4 us -> 22.4 us
  other arithmetic: 15.8 us -> 6.41 us
    dot_general x13 -> x0, matrix products: 41.7 us -> none  [the longest x1 11.1 us: body(): lax.dot_general(qkv_grad, w_qkv, (((1,), (1,)), ((), ())), preferred_elem...]
    pallas_call x0 -> x3, Pallas kernels: none -> 29.7 us  [the longest x1 11.6 us: body(): pl.pallas_call(block_kernel, grid=(HEADS,), out_shape=jax.ShapeDtypeStruc...]
    pallas_call x1, Pallas kernels: 158 us -> 141 us  [reduced_rows(): pl.pallas_call(functools.partial(reduce_kernel, seq_count, batch_count),...]
    ppermute x4, waiting for transfers between devices: 11.4 us -> 22.4 us  [swap(): lax.ppermute(value, 'seq', [(i, i ^ 1 << bit) for i in range(seq_count)])]
    unnamed x37 -> x4, local copies, waits for them, and re-layouts: 13 us -> 5.24 us
    reshape x4 -> x0, local copies, waits for them, and re-layouts: 7.49 us -> none  [the longest x1 2.28 us: body(): value_grad.reshape(row_count, width)]
    concatenate x1 -> x0, other arithmetic: 2.97 us -> none  [body(): jnp.concatenate([query_grad.reshape(row_count, width), key_grad.reshape(r...]
  transfers between devices with their start and end apart: 4 -> 4, of which waited for: 2 -> 3; matrix products, arithmetic and copies ran while one was open for 9% -> 2% of each run, Pallas kernels for 0% -> 5%
where the time goes in v2:
time: 225 us
  Pallas kernels  171 us (76%)
  waiting for transfers between devices  22.4 us (10%)
  matrix products  12.9 us (6%)
  other arithmetic  6.41 us (3%)
  local copies, waits for them, and re-layouts  6.39 us (3%)
  starting transfers between devices  5.31 us (2%)
    pallas_call x1, Pallas kernels, reduced_rows(): pl.pallas_call(functools.partial(reduce_kernel, seq_count, batch_count),...  141 us
    ppermute x4, waiting for transfers between devices, swap(): lax.ppermute(value, 'seq', [(i, i ^ 1 << bit) for i in range(seq_count)])  22.4 us
    dot_general x1, matrix products, body(): jnp.dot(local_x, w_qkv, preferred_element_type=jnp.float32)  12.9 us
    pallas_call x1, Pallas kernels, body(): pl.pallas_call(block_kernel, grid=(HEADS,), out_shape=jax.ShapeDtypeStruc...  11.6 us
    pallas_call x1, Pallas kernels, body(): pl.pallas_call(carry_kernel, grid=(HEADS,), out_shape=(jax.ShapeDtypeStru...  10.7 us
    pallas_call x1, Pallas kernels, body(): pl.pallas_call(state_kernel, grid=(HEADS,), out_shape=(jax.ShapeDtypeStru...  7.44 us
    ppermute x4, starting transfers between devices, swap(): lax.ppermute(value, 'seq', [(i, i ^ 1 << bit) for i in range(seq_count)])  5.31 us
    unnamed x4, local copies, waits for them, and re-layouts  5.24 us
  transfers between devices with their start and end apart: 4, of which 3 were waited for; matrix products, arithmetic and copies ran while one was open for 2% of the time, Pallas kernels for 5%

profile of v2, /device:TPU:0, one launch (start us, length us, event | category | flops | bytes accessed | tf_op | source)
XLA Modules:
  0.0 224.8 jit_solution(15963965876573234068)
XLA Ops:
  0.6 0.7 rsqrt_multiply_fusion.s_ref
  1.4 12.9 %convolution_convert_fusion.q_ref.k_ref.v_ref = bf16[512,3072]{1,0:T(8,128)(2,1)} fusion(bf16[2048,3072]{1,0:T(8,128)(2,1)} %w_hbm.1, bf16[1,512,2048]{2,1,0:T(8,128)(2,1)} %param.3), kind=kOutput, calls=%fused_computation | convolution fusion | flops 6444023808 | bytes 17825792 | tf_op jit(solution)/shard_map/dot_general | solution.py:342
  14.3 7.4 %shard_map.58 = (bf16[512,1024]{1,0:T(8,128)(2,1)}, f32[2,8,128,128]{3,2,1,0:T(8,128)}) custom-call(bf16[512,3072]{1,0:T(8,128)(2,1)} %convolution_convert_fusion.q_ref.k_ref.v_ref, bf16[512,3072]{1,0:T(8,128)(2,1)} %convolution_convert_fusion.q_ref.k_ref.v_ref, bf16[512,3072]{1,0:T(8,128)(2,1)} %convolution_convert_fusion.q_ref.k_ref.v_ref, ...), custom_call_target="tpu_custom_call" | custom-call | flops 268435456 | bytes 5242880 | tf_op jit(solution)/shard_map/pallas_call | solution.py:350
  21.7 0.5 collective-permute-start
  22.2 2.5 %collective-permute-done = f32[2,8,128,128]{3,2,1,0:T(8,128)S(1)} collective-permute-done((f32[2,8,128,128]{3,2,1,0:T(8,128)}, f32[2,8,128,128]{3,2,1,0:T(8,128)S(1)}, u32[]{:S(2)}, u32[]{:S(2)}) %collective-permute-start) | collective-permute-done | bytes 1048608 | tf_op jit(solution)/shard_map/ppermute | solution.py:31
  24.7 1.1 dynamic-slice_add_fusion
  25.8 2.9 %collective-permute-start.1 = (f32[2,4,128,128]{3,2,1,0:T(8,128)S(1)}, f32[2,4,128,128]{3,2,1,0:T(8,128)S(1)}, u32[]{:S(2)}, u32[]{:S(2)}) collective-permute-start(f32[2,4,128,128]{3,2,1,0:T(8,128)S(1)} %dynamic-slice_add_fusion), channel_id=1, source_target_pairs={{0,8},{4,12},{8,0},{12,4},{16,24},{20,28},{24,16},{28,20},{1,9},{5... | collective-permute-start | bytes 1572872 | tf_op jit(solution)/shard_map/ppermute | solution.py:31
  28.7 12.2 %collective-permute-done.1 = f32[2,4,128,128]{3,2,1,0:T(8,128)S(1)} collective-permute-done((f32[2,4,128,128]{3,2,1,0:T(8,128)S(1)}, f32[2,4,128,128]{3,2,1,0:T(8,128)S(1)}, u32[]{:S(2)}, u32[]{:S(2)}) %collective-permute-start.1) | collective-permute-done | bytes 524320 | tf_op jit(solution)/shard_map/ppermute | solution.py:31
  40.9 0.1 add.47
  41.0 1.8 collective-permute-start.2
  42.9 3.9 %copy.7 = bf16[1,512,2048]{1,2,0:T(8,128)(2,1)} copy(bf16[1,512,2048]{2,1,0:T(8,128)(2,1)} %param.3) | data formatting | bytes 4194304 | tf_op args[0]
  46.8 7.7 %collective-permute-done.2 = f32[2,4,128,128]{3,2,1,0:T(8,128)S(1)} collective-permute-done((f32[2,4,128,128]{3,2,1,0:T(8,128)S(1)}, f32[2,4,128,128]{3,2,1,0:T(8,128)S(1)}, u32[]{:S(2)}, u32[]{:S(2)}) %collective-permute-start.2) | collective-permute-done | bytes 524320 | tf_op jit(solution)/shard_map/ppermute | solution.py:31
  54.5 0.1 maximum_add_fusion.1
  54.6 0.1 collective-permute-start.3
  54.7 11.6 %shard_map.59.part_ref = f32[4,512,1024]{2,1,0:T(8,128)} custom-call(bf16[512,3072]{1,0:T(8,128)(2,1)} %convolution_convert_fusion.q_ref.k_ref.v_ref, bf16[512,3072]{1,0:T(8,128)(2,1)} %convolution_convert_fusion.q_ref.k_ref.v_ref, bf16[512,3072]{1,0:T(8,128)(2,1)} %convolution_convert_fusion.q_ref.k_ref.v_ref, bf16[512,1024]{1,0:T(8,128)(2,1)} %get-tuple-element.9.g_ref), custom_call_target="tpu_custom_call" | custom-call | flops 3221225472 | bytes 12582912 | tf_op jit(solution)/shard_map/pallas_call | solution.py:363
  66.3 0.1 slice_select_fusion.1
  66.4 0.0 collective-permute-done.3
  66.4 0.1 broadcast_select_fusion.1
  66.5 0.1 maximum_add_fusion
  66.6 1.2 slice_bitcast_fusion
  67.8 10.7 %shard_map.60 = (bf16[512,1024]{1,0:T(8,128)(2,1)}, bf16[512,3072]{1,0:T(8,128)(2,1)}) custom-call(bf16[512,3072]{1,0:T(8,128)(2,1)} %convolution_convert_fusion.q_ref.k_ref.v_ref, bf16[512,3072]{1,0:T(8,128)(2,1)} %convolution_convert_fusion.q_ref.k_ref.v_ref, bf16[512,3072]{1,0:T(8,128)(2,1)} %convolution_convert_fusion.q_ref.k_ref.v_ref, ...), custom_call_target="tpu_custom_call" | custom-call | flops 1073741824 | bytes 16777216 | tf_op jit(solution)/shard_map/pallas_call | solution.py:374
  78.5 140.9 %shard_map.61 = (f32[256,3072]{1,0:T(8,128)}, bf16[512,2048]{1,0:T(8,128)(2,1)}) custom-call(bf16[2048,512]{1,0:T(8,128)(2,1)} %bitcast.14, bf16[512,3072]{1,0:T(8,128)(2,1)} %get-tuple-element.12.g_ref, bf16[2048,3072]{1,0:T(8,128)(2,1)} %w_hbm.1), custom_call_target="tpu_custom_call" | custom-call | flops 12884901888 | bytes 25165824 | tf_op jit(solution)/shard_map/pallas_call | solution.py:260
  219.4 0.0 copy-start
  219.4 4.1 %broadcast_multiply_fusion = f32[256,3072]{1,0:T(8,128)} fusion(f32[256,3072]{1,0:T(8,128)} %get-tuple-element.14), kind=kLoop, calls=%fused_computation.2 | loop fusion | flops 786432 | bytes 6291456 | tf_op jit(solution)/shard_map/mul | solution.py:389
  223.4 0.0 copy-done
  223.4 1.3 copy.10
  (2 shorter events, 0.1 us)
Async XLA Ops:
  21.7 3.0 %collective-permute-start = (f32[2,8,128,128]{3,2,1,0:T(8,128)}, f32[2,8,128,128]{3,2,1,0:T(8,128)S(1)}, u32[]{:S(2)}, u32[]{:S(2)}) collective-permute-start(f32[2,8,128,128]{3,2,1,0:T(8,128)} %get-tuple-element.10), channel_id=1, source_target_pairs={{0,4},{4,0},{8,12},{12,8},{16,20},{20,16},{24,28},{28,24},{1,5},{5... | collective-permute-start | bytes 3145736 | tf_op jit(solution)/shard_map/ppermute | solution.py:31
  25.8 15.1 %collective-permute-start.1 = (f32[2,4,128,128]{3,2,1,0:T(8,128)S(1)}, f32[2,4,128,128]{3,2,1,0:T(8,128)S(1)}, u32[]{:S(2)}, u32[]{:S(2)}) collective-permute-start(f32[2,4,128,128]{3,2,1,0:T(8,128)S(1)} %dynamic-slice_add_fusion), channel_id=1, source_target_pairs={{0,8},{4,12},{8,0},{12,4},{16,24},{20,28},{24,16},{28,20},{1,9},{5... | collective-permute-start | bytes 1572872 | tf_op jit(solution)/shard_map/ppermute | solution.py:31
  41.0 13.5 %collective-permute-start.2 = (f32[2,4,128,128]{3,2,1,0:T(8,128)S(1)}, f32[2,4,128,128]{3,2,1,0:T(8,128)S(1)}, u32[]{:S(2)}, u32[]{:S(2)}) collective-permute-start(f32[2,4,128,128]{3,2,1,0:T(8,128)S(1)} %add.47), channel_id=1, source_target_pairs={{0,16},{4,20},{8,24},{12,28},{16,0},{20,4},{24,8},{28,12},{1,17},{... | collective-permute-start | bytes 1572872 | tf_op jit(solution)/shard_map/ppermute | solution.py:31
  54.6 11.8 %collective-permute-start.3 = (f32[2,4,128,128]{3,2,1,0:T(8,128)S(1)}, f32[2,4,128,128]{3,2,1,0:T(8,128)S(1)}, u32[]{:S(2)}, u32[]{:S(2)}) collective-permute-start(f32[2,4,128,128]{3,2,1,0:T(8,128)S(1)} %maximum_add_fusion.1), channel_id=1, source_target_pairs={{0,4},{4,0},{8,12},{12,8},{16,20},{20,16},{24,28},{28,24},{1,5},{5... | collective-permute-start | bytes 1572872 | tf_op jit(solution)/shard_map/ppermute | solution.py:31
  219.4 4.1 %copy-start = (bf16[512,2048]{1,0:T(8,128)(2,1)S(1)}, bf16[512,2048]{1,0:T(8,128)(2,1)}, u32[]{:S(2)}) copy-start(bf16[512,2048]{1,0:T(8,128)(2,1)} %get-tuple-element.13) | copy-start | bytes 6291460

commit v3 on v2

--- a/solution.py
+++ b/solution.py
@@ -22,7 +22,7 @@
     return bits
 
 
-def carries(own, seq_count):
+def carries(own, seq_count, work):
     bits = bits_of(seq_count)
     rank = lax.axis_index("seq")
     half = own.shape[1] // 2
@@ -38,15 +38,26 @@
     near = sides(other, 0)
     total = lax.dynamic_slice_in_dim(own + other, (rank & 1) * half, half, 1)
     far = jnp.zeros_like(total)
+    done = None
     for bit in range(1, bits):
-        other = swap(total, bit)
-        far = far + sides(other, bit)
-        total = total + other
+        upper = ((rank >> bit) & 1) == 1
+        last = bit == bits - 1
+        other = swap(jnp.where(upper, total[1], total[0]) if last else total, bit)
+        if bit == 1:
+            done = work(total)
+            other, done = lax.optimization_barrier((other, done))
+        if last:
+            far = far + jnp.stack([jnp.where(upper, other, 0.0), jnp.where(upper, 0.0, other)])
+        else:
+            far = far + sides(other, bit)
+            total = total + other
+    if done is None:
+        done = work(total)
     mate = swap(far, 0)
     low = (rank & 1) == 0
     joined = jnp.concatenate([jnp.where(low, far, mate), jnp.where(low, mate, far)], 1)
     result = near + joined
-    return result[0], result[1]
+    return result[0], result[1], done
 
 
 def orders(bits):
@@ -360,7 +371,7 @@
             flops=4 * row_count * width * DH, bytes_accessed=10 * row_count * width, transcendentals=0
         ),
     )(projected, projected, projected, cotangent[0], pos_scale)
-    parts = pl.pallas_call(
+    in_block = pl.pallas_call(
         block_kernel,
         grid=(HEADS,),
         out_shape=jax.ShapeDtypeStruct((4, row_count, width), jnp.float32),
@@ -369,8 +380,13 @@
         cost_estimate=pl.CostEstimate(
             flops=12 * row_count * width * BLK, bytes_accessed=24 * row_count * width, transcendentals=0
         ),
-    )(projected, projected, projected, scaled_grad)
-    kv_in, grad_in = carries(states, seq_count)
+    )
+
+    def work(total):
+        gated, _ = lax.optimization_barrier((scaled_grad, total))
+        return in_block(projected, projected, projected, gated)
+
+    kv_in, grad_in, parts = carries(states, seq_count, work)
     attended, qkv_grad = pl.pallas_call(
         carry_kernel,
         grid=(HEADS,),

time: 225 us -> 212 us (0.942)
  waiting for transfers between devices: 22.4 us -> 9.11 us
    ppermute x4, waiting for transfers between devices: 22.4 us -> 9.11 us  [swap(): lax.ppermute(value, 'seq', [(i, i ^ 1 << bit) for i in range(seq_count)])]
where the time goes in v3:
time: 212 us; the launch traced here: 211 us
  Pallas kernels  171 us (81%)
  matrix products  12.9 us (6%)
  waiting for transfers between devices  9.11 us (4%)
  other arithmetic  6.43 us (3%)
  local copies, waits for them, and re-layouts  6.4 us (3%)
  starting transfers between devices  5.31 us (3%)
    pallas_call x1, Pallas kernels, reduced_rows(): pl.pallas_call(functools.partial(reduce_kernel, seq_count, batch_count),...  141 us
    dot_general x1, matrix products, body(): jnp.dot(local_x, w_qkv, preferred_element_type=jnp.float32)  12.9 us
    pallas_call x1, Pallas kernels, work(): return in_block(projected, projected, projected, gated)  11.6 us
    pallas_call x1, Pallas kernels, body(): pl.pallas_call(carry_kernel, grid=(HEADS,), out_shape=(jax.ShapeDtypeStru...  10.7 us
    ppermute x4, waiting for transfers between devices, swap(): lax.ppermute(value, 'seq', [(i, i ^ 1 << bit) for i in range(seq_count)])  9.11 us
    pallas_call x1, Pallas kernels, body(): pl.pallas_call(state_kernel, grid=(HEADS,), out_shape=(jax.ShapeDtypeStru...  7.44 us
    ppermute x4, starting transfers between devices, swap(): lax.ppermute(value, 'seq', [(i, i ^ 1 << bit) for i in range(seq_count)])  5.31 us
    unnamed x4, local copies, waits for them, and re-layouts  5.25 us
  transfers between devices with their start and end apart: 4, of which 3 were waited for; matrix products, arithmetic and copies ran while one was open for 2% of the time, Pallas kernels for 5%

profile of v3, /device:TPU:0, one launch (start us, length us, event | category | flops | bytes accessed | tf_op | source)
XLA Modules:
  0.0 211.5 jit_solution(9917637954590215815)
XLA Ops:
  0.6 0.7 rsqrt_multiply_fusion.s_ref
  1.4 12.9 %convolution_convert_fusion.q_ref.k_ref.v_ref = bf16[512,3072]{1,0:T(8,128)(2,1)} fusion(bf16[2048,3072]{1,0:T(8,128)(2,1)} %w_hbm.1, bf16[1,512,2048]{2,1,0:T(8,128)(2,1)} %param.3), kind=kOutput, calls=%fused_computation | convolution fusion | flops 6444023808 | bytes 17825792 | tf_op jit(solution)/shard_map/dot_general | solution.py:353
  14.3 7.4 %shard_map.58 = (bf16[512,1024]{1,0:T(8,128)(2,1)}, f32[2,8,128,128]{3,2,1,0:T(8,128)}) custom-call(bf16[512,3072]{1,0:T(8,128)(2,1)} %convolution_convert_fusion.q_ref.k_ref.v_ref, bf16[512,3072]{1,0:T(8,128)(2,1)} %convolution_convert_fusion.q_ref.k_ref.v_ref, bf16[512,3072]{1,0:T(8,128)(2,1)} %convolution_convert_fusion.q_ref.k_ref.v_ref, ...), custom_call_target="tpu_custom_call" | custom-call | flops 268435456 | bytes 5242880 | tf_op jit(solution)/shard_map/pallas_call | solution.py:361
  21.7 0.5 collective-permute-start
  22.2 2.5 %collective-permute-done = f32[2,8,128,128]{3,2,1,0:T(8,128)S(1)} collective-permute-done((f32[2,8,128,128]{3,2,1,0:T(8,128)}, f32[2,8,128,128]{3,2,1,0:T(8,128)S(1)}, u32[]{:S(2)}, u32[]{:S(2)}) %collective-permute-start) | collective-permute-done | bytes 1048608 | tf_op jit(solution)/shard_map/ppermute | solution.py:31
  24.7 1.1 dynamic-slice_add_fusion
  25.8 2.9 %collective-permute-start.1 = (f32[2,4,128,128]{3,2,1,0:T(8,128)S(1)}, f32[2,4,128,128]{3,2,1,0:T(8,128)S(1)}, u32[]{:S(2)}, u32[]{:S(2)}) collective-permute-start(f32[2,4,128,128]{3,2,1,0:T(8,128)S(1)} %dynamic-slice_add_fusion), channel_id=1, source_target_pairs={{0,8},{4,12},{8,0},{12,4},{16,24},{20,28},{24,16},{28,20},{1,9},{5... | collective-permute-start | bytes 1572872 | tf_op jit(solution)/shard_map/ppermute | solution.py:31
  28.7 11.6 %shard_map.59.part_ref = f32[4,512,1024]{2,1,0:T(8,128)} custom-call(bf16[512,3072]{1,0:T(8,128)(2,1)} %convolution_convert_fusion.q_ref.k_ref.v_ref, bf16[512,3072]{1,0:T(8,128)(2,1)} %convolution_convert_fusion.q_ref.k_ref.v_ref, bf16[512,3072]{1,0:T(8,128)(2,1)} %convolution_convert_fusion.q_ref.k_ref.v_ref, bf16[512,1024]{1,0:T(8,128)(2,1)} %get-tuple-element.14.g_ref), custom_call_target="tpu_custom_call" | custom-call | flops 3221225472 | bytes 12582912 | tf_op jit(solution)/shard_map/pallas_call | solution.py:387
  40.3 0.6 collective-permute-done.1
  40.9 0.1 add.47
  41.0 1.8 collective-permute-start.2
  42.9 6.0 %collective-permute-done.2 = f32[4,128,128]{2,1,0:T(8,128)S(1)} collective-permute-done((f32[4,128,128]{2,1,0:T(8,128)S(1)}, f32[4,128,128]{2,1,0:T(8,128)S(1)}, u32[]{:S(2)}, u32[]{:S(2)}) %collective-permute-start.2) | collective-permute-done | bytes 262176 | tf_op jit(solution)/shard_map/ppermute | solution.py:31
  48.9 0.1 maximum_add_fusion.1
  49.0 0.1 collective-permute-start.3
  49.1 3.9 %copy.7 = bf16[1,512,2048]{1,2,0:T(8,128)(2,1)} copy(bf16[1,512,2048]{2,1,0:T(8,128)(2,1)} %param.3) | data formatting | bytes 4194304 | tf_op args[0]
  53.0 0.1 slice_select_fusion.1
  53.1 0.0 collective-permute-done.3
  53.1 0.1 broadcast_select_fusion.1
  53.2 0.1 maximum_add_fusion
  53.3 1.2 slice_bitcast_fusion
  54.5 10.7 %shard_map.60 = (bf16[512,1024]{1,0:T(8,128)(2,1)}, bf16[512,3072]{1,0:T(8,128)(2,1)}) custom-call(bf16[512,3072]{1,0:T(8,128)(2,1)} %convolution_convert_fusion.q_ref.k_ref.v_ref, bf16[512,3072]{1,0:T(8,128)(2,1)} %convolution_convert_fusion.q_ref.k_ref.v_ref, bf16[512,3072]{1,0:T(8,128)(2,1)} %convolution_convert_fusion.q_ref.k_ref.v_ref, ...), custom_call_target="tpu_custom_call" | custom-call | flops 1073741824 | bytes 16777216 | tf_op jit(solution)/shard_map/pallas_call | solution.py:390
  65.2 140.8 %shard_map.61 = (f32[256,3072]{1,0:T(8,128)}, bf16[512,2048]{1,0:T(8,128)(2,1)}) custom-call(bf16[2048,512]{1,0:T(8,128)(2,1)} %bitcast.20, bf16[512,3072]{1,0:T(8,128)(2,1)} %get-tuple-element.18.g_ref, bf16[2048,3072]{1,0:T(8,128)(2,1)} %w_hbm.1), custom_call_target="tpu_custom_call" | custom-call | flops 12884901888 | bytes 25165824 | tf_op jit(solution)/shard_map/pallas_call | solution.py:271
  206.1 0.0 copy-start
  206.1 4.1 %broadcast_multiply_fusion = f32[256,3072]{1,0:T(8,128)} fusion(f32[256,3072]{1,0:T(8,128)} %get-tuple-element.20), kind=kLoop, calls=%fused_computation.2 | loop fusion | flops 786432 | bytes 6291456 | tf_op jit(solution)/shard_map/mul | solution.py:405
  210.1 0.0 copy-done
  210.1 1.3 copy.10
  (3 shorter events, 0.1 us)
Async XLA Ops:
  21.7 3.0 %collective-permute-start = (f32[2,8,128,128]{3,2,1,0:T(8,128)}, f32[2,8,128,128]{3,2,1,0:T(8,128)S(1)}, u32[]{:S(2)}, u32[]{:S(2)}) collective-permute-start(f32[2,8,128,128]{3,2,1,0:T(8,128)} %get-tuple-element.13), channel_id=1, source_target_pairs={{0,4},{4,0},{8,12},{12,8},{16,20},{20,16},{24,28},{28,24},{1,5},{5... | collective-permute-start | bytes 3145736 | tf_op jit(solution)/shard_map/ppermute | solution.py:31
  25.8 15.1 %collective-permute-start.1 = (f32[2,4,128,128]{3,2,1,0:T(8,128)S(1)}, f32[2,4,128,128]{3,2,1,0:T(8,128)S(1)}, u32[]{:S(2)}, u32[]{:S(2)}) collective-permute-start(f32[2,4,128,128]{3,2,1,0:T(8,128)S(1)} %dynamic-slice_add_fusion), channel_id=1, source_target_pairs={{0,8},{4,12},{8,0},{12,4},{16,24},{20,28},{24,16},{28,20},{1,9},{5... | collective-permute-start | bytes 1572872 | tf_op jit(solution)/shard_map/ppermute | solution.py:31
  41.0 7.8 %collective-permute-start.2 = (f32[4,128,128]{2,1,0:T(8,128)S(1)}, f32[4,128,128]{2,1,0:T(8,128)S(1)}, u32[]{:S(2)}, u32[]{:S(2)}) collective-permute-start(f32[4,128,128]{2,1,0:T(8,128)S(1)} %fusion.1), channel_id=1, source_target_pairs={{0,16},{4,20},{8,24},{12,28},{16,0},{20,4},{24,8},{28,12},{1,17},{... | collective-permute-start | bytes 786440 | tf_op jit(solution)/shard_map/ppermute | solution.py:31
  49.0 4.1 %collective-permute-start.3 = (f32[2,4,128,128]{3,2,1,0:T(8,128)S(1)}, f32[2,4,128,128]{3,2,1,0:T(8,128)S(1)}, u32[]{:S(2)}, u32[]{:S(2)}) collective-permute-start(f32[2,4,128,128]{3,2,1,0:T(8,128)S(1)} %maximum_add_fusion.1), channel_id=1, source_target_pairs={{0,4},{4,0},{8,12},{12,8},{16,20},{20,16},{24,28},{28,24},{1,5},{5... | collective-permute-start | bytes 1572872 | tf_op jit(solution)/shard_map/ppermute | solution.py:31
  206.1 4.1 %copy-start = (bf16[512,2048]{1,0:T(8,128)(2,1)S(1)}, bf16[512,2048]{1,0:T(8,128)(2,1)}, u32[]{:S(2)}) copy-start(bf16[512,2048]{1,0:T(8,128)(2,1)} %get-tuple-element.19) | copy-start | bytes 6291460
